TPU v7x, 32 devices: a whole 2x2x4 slice. The times are simulated.
32 devices in a mesh: grid: 16 (over z, y, x), band: 2 (over core).
Axes of the slice: x: 2, y: 2, z: 4, core: 2. Of those that a mesh axis runs over, the one named last changes fastest.
Arguments:
- orbitals: float32 [16, 16, 32, 32, 128], P('grid', 'band'), may hold values from -24 to 24, as said below
- potential: float32 [16, 32, 32, 128], P('grid'), may hold values from -1 to 1
Outputs:
- rotated: float32 [16, 16, 32, 32, 128], P('grid', 'band')
Inputs may be any that keep to these rules, and one draw needn't show every extreme that they name: `orbitals`: real-valued orbital samples.
All inputs are finite; a program needn't handle non-finite values.
Results may differ from a plain program's by a relative error of at most 0.00013.
Values sent between devices are 32-bit elements; how exact they have to be, the bound alone decides.
A program may use at most 128 MiB of HBM per device.

v0:
```python
import jax
import jax.numpy as jnp
from jax import lax
from jax.sharding import PartitionSpec as P

COEFFS = (-49.0 / 18.0, 1.5, -0.15, 1.0 / 90.0)
CENTER = 5.75
HALF_WIDTH = 4.75


def shifted(value, axis, steps):
    count = lax.axis_size(axis)
    leading, last = (max(0, -steps), min(count, count - steps))
    return lax.ppermute(value, axis, [(source, source + steps) for source in range(leading, last)])


def layout():
    devices_grid = lax.axis_size("grid")
    parts_x = max(2, devices_grid // 32)
    parts_z = devices_grid // (parts_x * parts_x)
    return (parts_x, parts_x, parts_z)


def neighbour(face_block, stride, keep_it):
    moved = shifted(face_block.reshape(face_block.shape[0], -1), "grid", stride)
    return jnp.where(keep_it, moved, 0.0).reshape(face_block.shape)


def apply_hamil(values_in, local_potential):
    parts_x, parts_y, parts_z = layout()
    grid_index = lax.axis_index("grid")
    pos_z = grid_index % parts_z
    pos_y = grid_index // parts_z % parts_y
    reach_max = len(COEFFS) - 1
    padded = jnp.pad(
        values_in, ((0, 0), (reach_max, reach_max), (reach_max, reach_max), (reach_max, reach_max))
    )
    plan = (
        (1, parts_y * parts_z, True, True),
        (2, parts_z, pos_y > 0, pos_y < parts_y - 1),
        (3, 1, pos_z > 0, pos_z < parts_z - 1),
    )
    for dim_index, stride, keep_lower, keep_upper in plan:
        extent = values_in.shape[dim_index]
        lower_face = neighbour(
            lax.slice_in_dim(values_in, extent - reach_max, extent, axis=dim_index),
            stride,
            keep_lower,
        )
        upper_face = neighbour(
            lax.slice_in_dim(values_in, 0, reach_max, axis=dim_index), -stride, keep_upper
        )
        lower_start = [0, reach_max, reach_max, reach_max]
        upper_start = [0, reach_max, reach_max, reach_max]
        lower_start[dim_index] = 0
        upper_start[dim_index] = reach_max + extent
        padded = lax.dynamic_update_slice(padded, lower_face, lower_start)
        padded = lax.dynamic_update_slice(padded, upper_face, upper_start)
    summed = 3.0 * COEFFS[0] * values_in
    for dim_index in range(1, 4):
        extent = values_in.shape[dim_index]
        for reach in range(1, reach_max + 1):
            upper_start = [0, reach_max, reach_max, reach_max]
            lower_start = [0, reach_max, reach_max, reach_max]
            upper_start[dim_index] = reach_max + reach
            lower_start[dim_index] = reach_max - reach
            upper_part = lax.slice(
                padded, upper_start, [upper_start[k] + values_in.shape[k] for k in range(4)]
            )
            lower_part = lax.slice(
                padded, lower_start, [lower_start[k] + values_in.shape[k] for k in range(4)]
            )
            summed = summed + COEFFS[reach] * (upper_part + lower_part)
    return -0.5 * summed + local_potential[None] * values_in


def chebyshev(start_block, local_potential):
    first_term = (apply_hamil(start_block, local_potential) - CENTER * start_block) / HALF_WIDTH
    return (
        2.0 * (apply_hamil(first_term, local_potential) - CENTER * first_term) / HALF_WIDTH
        - start_block
    )


def on_device(orbitals, potential):
    local_block = orbitals[0]
    local_potential = potential[0]
    band_index = lax.axis_index("band")
    local_count = local_block.shape[0]
    own_filtered = chebyshev(local_block, local_potential)
    gathered = lax.all_gather(own_filtered, "band", axis=0, tiled=True)
    total_orbs = gathered.shape[0]
    flat_all = gathered.reshape(total_orbs, -1)
    volume = flat_all.shape[1] * lax.axis_size("grid")
    partial_value = jnp.einsum("ic,jc->ij", flat_all, flat_all, precision=lax.Precision.HIGHEST)
    gram = lax.psum(partial_value, "grid")
    gram = gram / volume
    factor = jnp.linalg.cholesky(gram)
    weights = jax.scipy.linalg.solve_triangular(
        factor, jnp.eye(total_orbs, dtype=jnp.float32), lower=True
    )
    weight_rows = lax.dynamic_slice_in_dim(weights, band_index * local_count, local_count, 0)
    rotated = jnp.dot(
        weight_rows, flat_all, precision=lax.Precision.HIGHEST, preferred_element_type=jnp.float32
    )
    return rotated.reshape(local_block.shape)[None]


def solution(mesh):
    in_specs = (P("grid", "band", None, None, None), P("grid", None, None, None))
    out_specs = P("grid", "band", None, None, None)
    return jax.shard_map(
        on_device, mesh=mesh, in_specs=in_specs, out_specs=out_specs, check_vma=False
    )
```

profile of v0, /device:TPU:0, one launch (start us, length us, event | category | flops | bytes accessed | tf_op | source)
XLA Modules:
  0.0 975.7 jit_solution(6393854721621182004)
XLA Ops:
  6.5 6.0 copy.68
  12.5 1.0 fusion.61
  13.6 5.7 collective-permute-start.2
  20.2 4.5 collective-permute-start
  24.7 1.3 collective-permute-start.1
  26.0 1.3 collective-permute-start.3
  27.3 4.7 fusion.60
  32.0 8.5 copy.22
  40.6 1.7 reshape.98
  42.3 2.5 copy.23
  44.7 4.0 collective-permute-start.4
  48.9 9.1 pad.7
  58.0 8.5 copy.26
  66.5 1.6 reshape.100
  68.2 1.8 copy.27
  70.0 1.6 collective-permute-start.5
  71.6 6.2 reshape.117
  77.8 7.9 copy.25
  85.7 6.2 reshape.118
  91.9 17.1 %copy.29 = f32[8,32,32,3]{3,0,2,1:T(8,128)} copy(f32[8,32,32,3]{3,2,1,0:T(8,128)} %reshape.118) | data formatting | bytes 196608 | tf_op jit(solution)/shard_map/reshape | solution.py:26
  109.1 17.4 %dynamic_update_slice.36 = f32[8,38,38,134]{3,0,2,1:T(8,128)} dynamic-update-slice(f32[8,38,38,134]{3,0,2,1:T(8,128)} %pad.7, f32[8,3,32,128]{3,0,2,1:T(8,128)} %bitcast.2, s32[]{:T(128)} %constant.106.clone.1, s32[]{:T(128)} %constant.106.clone.1, s32[]{:T(128)} %constant.107.clone.1, s32[]{:T(128)} %constant.107.clone.1) | dynamic-update-slice | bytes 786436 | tf_op jit(solution)/shard_map/dynamic_update_slice | solution.py:57
  126.4 17.7 %dynamic_update_slice.37 = f32[8,38,38,134]{3,0,2,1:T(8,128)} dynamic-update-slice(f32[8,38,38,134]{3,0,2,1:T(8,128)} %dynamic_update_slice.36, f32[8,3,32,128]{3,0,2,1:T(8,128)S(1)} %bitcast.78, s32[]{:T(128)} %constant.106.clone.1, s32[]{:T(128)} %constant.108.clone.1, s32[]{:T(128)} %constant.107.clone.1, s32[]{:T(128)} %constant.107.clone.1) | dynamic-update-slice | bytes 786436 | tf_op jit(solution)/shard_map/dynamic_update_slice | solution.py:58
  144.1 17.8 %dynamic_update_slice.38 = f32[8,38,38,134]{3,0,2,1:T(8,128)} dynamic-update-slice(f32[8,38,38,134]{3,0,2,1:T(8,128)} %dynamic_update_slice.37, f32[8,32,3,128]{3,0,2,1:T(8,128)S(1)} %bitcast.75, s32[]{:T(128)} %constant.106.clone.1, s32[]{:T(128)} %constant.107.clone.1, s32[]{:T(128)} %constant.106.clone.1, s32[]{:T(128)} %constant.107.clone.1) | dynamic-update-slice | bytes 786436 | tf_op jit(solution)/shard_map/dynamic_update_slice | solution.py:57
  163.0 17.9 %dynamic_update_slice.39 = f32[8,38,38,134]{3,0,2,1:T(8,128)} dynamic-update-slice(f32[8,38,38,134]{3,0,2,1:T(8,128)} %dynamic_update_slice.38, f32[8,32,3,128]{3,0,2,1:T(8,128)S(1)} %bitcast.77, s32[]{:T(128)} %constant.106.clone.1, s32[]{:T(128)} %constant.107.clone.1, s32[]{:T(128)} %constant.108.clone.1, s32[]{:T(128)} %constant.107.clone.1) | dynamic-update-slice | bytes 786436 | tf_op jit(solution)/shard_map/dynamic_update_slice | solution.py:58
  180.8 28.3 %dynamic_update_slice.40 = f32[8,38,38,134]{3,0,2,1:T(8,128)} dynamic-update-slice(f32[8,38,38,134]{3,0,2,1:T(8,128)} %dynamic_update_slice.39, f32[8,32,32,3]{3,0,2,1:T(8,128)} %copy.25, s32[]{:T(128)} %constant.106.clone.1, s32[]{:T(128)} %constant.107.clone.1, s32[]{:T(128)} %constant.107.clone.1, s32[]{:T(128)} %constant.106.clone.1) | dynamic-update-slice | bytes 196612 | tf_op jit(solution)/shard_map/dynamic_update_slice | solution.py:57
  209.1 163.7 %dynamic_update_slice.41 = f32[8,38,38,134]{3,0,2,1:T(8,128)} dynamic-update-slice(f32[8,38,38,134]{3,0,2,1:T(8,128)} %dynamic_update_slice.40, f32[8,32,32,3]{3,0,2,1:T(8,128)} %copy.29, s32[]{:T(128)} %constant.106.clone.1, s32[]{:T(128)} %constant.107.clone.1, s32[]{:T(128)} %constant.107.clone.1, s32[]{:T(128)} %constant.115.clone.1) | dynamic-update-slice | bytes 196612 | tf_op jit(solution)/shard_map/dynamic_update_slice | solution.py:58
  372.8 61.8 %broadcast_multiply_fusion = (f32[8,32,32,128]{3,0,2,1:T(8,128)}, f32[8,32,32,128]{3,0,2,1:T(8,128)}) fusion(f32[32,32,128]{2,1,0:T(8,128)S(1)} %bitcast.73, f32[8,38,38,134]{3,0,2,1:T(8,128)} %dynamic_update_slice.41, f32[1,8,32,32,128]{4,3,2,1,0:T(8,128)} %param.2), kind=kLoop, calls=%fused_computation.67 | loop fusion | flops 35651584 | bytes 88604672 | tf_op jit(solution)/shard_map/div | solution.py:78
  434.6 2.1 fusion.59
  436.7 7.9 fusion.57
  444.7 8.5 copy.30
  453.2 2.1 reshape.110
  455.3 1.8 copy.31
  457.1 6.1 collective-permute-start.10
  463.2 2.1 fusion.58
  465.3 9.1 pad.8
  474.4 4.9 collective-permute-start.6
  479.3 1.3 collective-permute-start.7
  480.6 5.4 collective-permute-start.8
  486.0 1.3 collective-permute-start.9
  487.3 8.6 copy.34
  495.9 1.6 reshape.112
  497.5 1.8 copy.35
  499.3 1.3 collective-permute-start.11
  500.7 6.2 reshape.119
  506.9 8.0 copy.33
  514.8 6.2 reshape.120
  521.0 8.1 copy.37
  529.2 17.7 %dynamic_update_slice.42 = f32[8,38,38,134]{3,0,2,1:T(8,128)} dynamic-update-slice(f32[8,38,38,134]{3,0,2,1:T(8,128)} %pad.8, f32[8,3,32,128]{3,0,2,1:T(8,128)S(1)} %bitcast.80, s32[]{:T(128)} %constant.106.clone.1, s32[]{:T(128)} %constant.106.clone.1, s32[]{:T(128)} %constant.107.clone.1, s32[]{:T(128)} %constant.107.clone.1) | dynamic-update-slice | bytes 786436 | tf_op jit(solution)/shard_map/dynamic_update_slice | solution.py:57
  546.9 17.7 %dynamic_update_slice.43 = f32[8,38,38,134]{3,0,2,1:T(8,128)} dynamic-update-slice(f32[8,38,38,134]{3,0,2,1:T(8,128)} %dynamic_update_slice.42, f32[8,3,32,128]{3,0,2,1:T(8,128)S(1)} %bitcast.79, s32[]{:T(128)} %constant.106.clone.1, s32[]{:T(128)} %constant.108.clone.1, s32[]{:T(128)} %constant.107.clone.1, s32[]{:T(128)} %constant.107.clone.1) | dynamic-update-slice | bytes 786436 | tf_op jit(solution)/shard_map/dynamic_update_slice | solution.py:58
  564.6 17.8 %dynamic_update_slice.44 = f32[8,38,38,134]{3,0,2,1:T(8,128)} dynamic-update-slice(f32[8,38,38,134]{3,0,2,1:T(8,128)} %dynamic_update_slice.43, f32[8,32,3,128]{3,0,2,1:T(8,128)S(1)} %bitcast.74, s32[]{:T(128)} %constant.106.clone.1, s32[]{:T(128)} %constant.107.clone.1, s32[]{:T(128)} %constant.106.clone.1, s32[]{:T(128)} %constant.107.clone.1) | dynamic-update-slice | bytes 786436 | tf_op jit(solution)/shard_map/dynamic_update_slice | solution.py:57
  583.5 17.9 %dynamic_update_slice.45 = f32[8,38,38,134]{3,0,2,1:T(8,128)} dynamic-update-slice(f32[8,38,38,134]{3,0,2,1:T(8,128)} %dynamic_update_slice.44, f32[8,32,3,128]{3,0,2,1:T(8,128)S(1)} %bitcast.76, s32[]{:T(128)} %constant.106.clone.1, s32[]{:T(128)} %constant.107.clone.1, s32[]{:T(128)} %constant.108.clone.1, s32[]{:T(128)} %constant.107.clone.1) | dynamic-update-slice | bytes 786436 | tf_op jit(solution)/shard_map/dynamic_update_slice | solution.py:58
  601.3 28.3 %dynamic_update_slice.46 = f32[8,38,38,134]{3,0,2,1:T(8,128)} dynamic-update-slice(f32[8,38,38,134]{3,0,2,1:T(8,128)} %dynamic_update_slice.45, f32[8,32,32,3]{3,0,2,1:T(8,128)} %copy.33, s32[]{:T(128)} %constant.106.clone.1, s32[]{:T(128)} %constant.107.clone.1, s32[]{:T(128)} %constant.107.clone.1, s32[]{:T(128)} %constant.106.clone.1) | dynamic-update-slice | bytes 196612 | tf_op jit(solution)/shard_map/dynamic_update_slice | solution.py:57
  629.6 163.7 %dynamic_update_slice.47 = f32[8,38,38,134]{3,0,2,1:T(8,128)} dynamic-update-slice(f32[8,38,38,134]{3,0,2,1:T(8,128)} %dynamic_update_slice.46, f32[8,32,32,3]{3,0,2,1:T(8,128)} %copy.37, s32[]{:T(128)} %constant.106.clone.1, s32[]{:T(128)} %constant.107.clone.1, s32[]{:T(128)} %constant.107.clone.1, s32[]{:T(128)} %constant.115.clone.1) | dynamic-update-slice | bytes 196612 | tf_op jit(solution)/shard_map/dynamic_update_slice | solution.py:58
  793.3 62.5 %fusion.8 = f32[8,32,32,128]{3,0,2,1:T(8,128)} fusion(f32[8,38,38,134]{3,0,2,1:T(8,128)} %dynamic_update_slice.47, f32[8,32,32,128]{3,0,2,1:T(8,128)} %get-tuple-element.6, f32[32,32,128]{2,1,0:T(8,128)S(1)} %broadcast_multiply_fusion.1, f32[1,8,32,32,128]{4,3,2,1,0:T(8,128)} %param.2), kind=kLoop, calls=%fused_computation.10 | loop fusion | flops 36700160 | bytes 88604672 | tf_op jit(solution)/shard_map/sub | solution.py:80
  855.8 24.7 %all-gather.2.cloned.1.call-done = f32[16,32,32,128]{3,0,2,1:T(8,128)} async-done(((f32[8,32,32,128]{3,0,2,1:T(8,128)}), f32[16,32,32,128]{3,0,2,1:T(8,128)}) %all-gather.2.cloned.1.call-update) | async-done | bytes 8388624 | tf_op jit(solution)/shard_map/all_gather | solution.py:91
  880.5 16.6 %convolution_bitcast_fusion = f32[16,16]{0,1:T(8,128)S(1)} fusion(f32[16,32,32,128]{3,0,2,1:T(8,128)} %all-gather.2.cloned.1.call-done), kind=kOutput, calls=%fused_computation.68 | convolution fusion | flops 402653184 | bytes 8389632 | tf_op jit(solution)/shard_map/ic,jc->ij/dot_general | solution.py:95
  897.0 42.7 %psum.7 = f32[16,16]{0,1:T(8,128)S(1)} all-reduce(f32[16,16]{0,1:T(8,128)S(1)} %convolution_bitcast_fusion), channel_id=1, replica_groups=mesh['grid'=16,'band'=2] {'grid'}, use_global_device_ids=true, to_apply=%region_0.1 | all-reduce | flops 256 | bytes 2048 | tf_op jit(solution)/shard_map/psum | solution.py:96
  939.8 1.5 cholesky.17
  942.6 1.2 custom-call.7
  944.1 6.1 copy.40
  950.2 4.9 copy.67
  955.0 1.6 copy.55
  956.6 9.0 fusion.46
  965.7 2.8 copy.42
  (35 shorter events, 4.8 us)
Async XLA Ops:
  6.5 873.9 %all-gather.2.cloned.1.call-start = ((), (), s32[]{:S(2)}) async-start(), calls=%async_computation | async-start | bytes 12582912 | tf_op jit(solution)/shard_map/all_gather | solution.py:91
  12.5 19.5 %copy-start = (f32[1,8,32,32,128]{4,1,3,2,0:T(8,128)}, f32[1,8,32,32,128]{4,1,3,2,0:T(8,128)S(1)}, u32[]{:S(2)}) copy-start(f32[1,8,32,32,128]{4,1,3,2,0:T(8,128)S(1)} %copy.68) | copy-start | bytes 12582916
  13.6 95.4 %collective-permute-start.2 = (f32[8,12288]{1,0:T(8,128)}, f32[8,12288]{1,0:T(8,128)}, u32[]{:S(2)}, u32[]{:S(2)}) collective-permute-start(f32[8,12288]{1,0:T(8,128)} %bitcast.5), channel_id=1, source_target_pairs={{0,8},{2,10},{4,12},{6,14},{8,16},{10,18},{12,20},{14,22},{16,24},... | collective-permute-start | bytes 1179656 | tf_op jit(solution)/shard_map/ppermute | solution.py:14
  20.2 88.9 %collective-permute-start = (f32[8,12288]{1,0:T(8,128)}, f32[8,12288]{1,0:T(8,128)}, u32[]{:S(2)}, u32[]{:S(2)}) collective-permute-start(f32[8,12288]{1,0:T(8,128)} %bitcast.1), channel_id=1, source_target_pairs={{0,16},{2,18},{4,20},{6,22},{8,24},{10,26},{12,28},{14,30},{1,17},... | collective-permute-start | bytes 1179656 | tf_op jit(solution)/shard_map/ppermute | solution.py:14
  24.7 101.7 %collective-permute-start.1 = (f32[8,12288]{1,0:T(8,128)}, f32[8,12288]{1,0:T(8,128)S(1)}, u32[]{:S(2)}, u32[]{:S(2)}) collective-permute-start(f32[8,12288]{1,0:T(8,128)} %bitcast.3), channel_id=1, source_target_pairs={{16,0},{18,2},{20,4},{22,6},{24,8},{26,10},{28,12},{30,14},{17,1},... | collective-permute-start | bytes 1179656 | tf_op jit(solution)/shard_map/ppermute | solution.py:14
  26.0 136.0 %collective-permute-start.3 = (f32[8,12288]{1,0:T(8,128)}, f32[8,12288]{1,0:T(8,128)}, u32[]{:S(2)}, u32[]{:S(2)}) collective-permute-start(f32[8,12288]{1,0:T(8,128)} %bitcast.7), channel_id=1, source_target_pairs={{8,0},{10,2},{12,4},{14,6},{16,8},{18,10},{20,12},{22,14},{24,16},... | collective-permute-start | bytes 1179656 | tf_op jit(solution)/shard_map/ppermute | solution.py:14
  40.6 8.2 copy-start.1
  44.7 25.3 %collective-permute-start.4 = (f32[8,3072]{1,0:T(8,128)}, f32[8,3072]{1,0:T(8,128)}, u32[]{:S(2)}, u32[]{:S(2)}) collective-permute-start(f32[8,3072]{1,0:T(8,128)} %copy.23), channel_id=1, source_target_pairs={{0,2},{2,4},{4,6},{6,8},{8,10},{10,12},{12,14},{14,16},{16,18},{18... | collective-permute-start | bytes 294920 | tf_op jit(solution)/shard_map/ppermute | solution.py:14
  70.0 15.7 %collective-permute-start.5 = (f32[8,3072]{1,0:T(8,128)S(1)}, f32[8,3072]{1,0:T(8,128)S(1)}, u32[]{:S(2)}, u32[]{:S(2)}) collective-permute-start(f32[8,3072]{1,0:T(8,128)S(1)} %copy.27), channel_id=1, source_target_pairs={{2,0},{4,2},{6,4},{8,6},{10,8},{12,10},{14,12},{16,14},{18,16},{20... | collective-permute-start | bytes 294920 | tf_op jit(solution)/shard_map/ppermute | solution.py:14
  457.1 42.2 %collective-permute-start.10 = (f32[8,3072]{1,0:T(8,128)S(1)}, f32[8,3072]{1,0:T(8,128)}, u32[]{:S(2)}, u32[]{:S(2)}) collective-permute-start(f32[8,3072]{1,0:T(8,128)S(1)} %copy.31), channel_id=1, source_target_pairs={{0,2},{2,4},{4,6},{6,8},{8,10},{10,12},{12,14},{14,16},{16,18},{18... | collective-permute-start | bytes 294920 | tf_op jit(solution)/shard_map/ppermute | solution.py:14
  474.4 54.8 %collective-permute-start.6 = (f32[8,12288]{1,0:T(8,128)}, f32[8,12288]{1,0:T(8,128)S(1)}, u32[]{:S(2)}, u32[]{:S(2)}) collective-permute-start(f32[8,12288]{1,0:T(8,128)} %bitcast.10), channel_id=1, source_target_pairs={{0,16},{2,18},{4,20},{6,22},{8,24},{10,26},{12,28},{14,30},{1,17},... | collective-permute-start | bytes 1179656 | tf_op jit(solution)/shard_map/ppermute | solution.py:14
  479.3 67.7 %collective-permute-start.7 = (f32[8,12288]{1,0:T(8,128)}, f32[8,12288]{1,0:T(8,128)S(1)}, u32[]{:S(2)}, u32[]{:S(2)}) collective-permute-start(f32[8,12288]{1,0:T(8,128)} %bitcast.12), channel_id=1, source_target_pairs={{16,0},{18,2},{20,4},{22,6},{24,8},{26,10},{28,12},{30,14},{17,1},... | collective-permute-start | bytes 1179656 | tf_op jit(solution)/shard_map/ppermute | solution.py:14
  480.6 48.6 %collective-permute-start.8 = (f32[8,12288]{1,0:T(8,128)}, f32[8,12288]{1,0:T(8,128)}, u32[]{:S(2)}, u32[]{:S(2)}) collective-permute-start(f32[8,12288]{1,0:T(8,128)} %bitcast.14), channel_id=1, source_target_pairs={{0,8},{2,10},{4,12},{6,14},{8,16},{10,18},{12,20},{14,22},{16,24},... | collective-permute-start | bytes 1179656 | tf_op jit(solution)/shard_map/ppermute | solution.py:14
  486.0 96.4 %collective-permute-start.9 = (f32[8,12288]{1,0:T(8,128)}, f32[8,12288]{1,0:T(8,128)}, u32[]{:S(2)}, u32[]{:S(2)}) collective-permute-start(f32[8,12288]{1,0:T(8,128)} %bitcast.16), channel_id=1, source_target_pairs={{8,0},{10,2},{12,4},{14,6},{16,8},{18,10},{20,12},{22,14},{24,16},... | collective-permute-start | bytes 1179656 | tf_op jit(solution)/shard_map/ppermute | solution.py:14
  499.3 15.5 %collective-permute-start.11 = (f32[8,3072]{1,0:T(8,128)S(1)}, f32[8,3072]{1,0:T(8,128)S(1)}, u32[]{:S(2)}, u32[]{:S(2)}) collective-permute-start(f32[8,3072]{1,0:T(8,128)S(1)} %copy.35), channel_id=1, source_target_pairs={{2,0},{4,2},{6,4},{8,6},{10,8},{12,10},{14,12},{16,14},{18,16},{20... | collective-permute-start | bytes 294920 | tf_op jit(solution)/shard_map/ppermute | solution.py:14
Sparse Core Ops, SparseCore 0:
  855.9 24.4 all-gather.1
where the time goes:
time: 986 us; the launch traced here: 976 us
  local copies, waits for them, and re-layouts  699 us (71%)
  other arithmetic  130 us (13%)
  blocking collectives  42.7 us (4%)
  starting transfers between devices  38.6 us (4%)
  matrix products  25.8 us (3%)
  waiting for transfers between devices  24.7 us (3%)
  between operations  14.2 us (1%)
    dynamic_update_slice x6, local copies, waits for them, and re-layouts, apply_hamil(): padded = lax.dynamic_update_slice(padded, upper_face, upper_start)  398 us
    dynamic_update_slice x6, local copies, waits for them, and re-layouts, apply_hamil(): padded = lax.dynamic_update_slice(padded, lower_face, lower_start)  127 us
    reshape x8, local copies, waits for them, and re-layouts, neighbour(): return jnp.where(keep_it, moved, 0.0).reshape(face_block.shape)  65.9 us
    sub x1, other arithmetic, chebyshev(): 2.0 * (apply_hamil(first_term, local_potential) - CENTER * first_term)  62.5 us
    div x1, other arithmetic, chebyshev(): (apply_hamil(start_block, local_potential) - CENTER * start_block) / HALF...  61.8 us
    psum x1, blocking collectives, on_device(): gram = lax.psum(partial_value, 'grid')  42.7 us
    ppermute x12, starting transfers between devices, shifted(): lax.ppermute(value, axis, [(source, source + steps) for source in range(l...  38.6 us
    slice x8, local copies, waits for them, and re-layouts, apply_hamil(): lax.slice_in_dim(values_in, 0, reach_max, axis=dim_index)  36 us
  transfers between devices with their start and end apart: 13, of which 1 were waited for; matrix products, arithmetic and copies ran while one was open for 24% of the time, Pallas kernels for 0%

commit v1 on v0

v1 whole, which is shorter than its diff:
```python
import functools

import jax
import jax.numpy as jnp
from jax import lax
from jax.experimental import pallas as pl
from jax.experimental.pallas import tpu as pltpu
from jax.sharding import PartitionSpec as P

COEFFS = (-49.0 / 18.0, 1.5, -0.15, 1.0 / 90.0)
CENTER = 5.75
HALF_WIDTH = 4.75
TAPS = tuple(-0.5 * c / HALF_WIDTH for c in COEFFS)
DIAGONAL = 3.0 * -0.5 * COEFFS[0] - CENTER
REACH = 3
LEAD = 8
UNROLL = 4
SLOT = 8
F32, BF16 = jnp.float32, jnp.bfloat16
HIGHEST = lax.Precision.HIGHEST
MESH = pl.DeviceIdType.MESH


def layout(devices_grid):
    parts_x = max(2, devices_grid // 32)
    return (parts_x, parts_x, devices_grid // (parts_x * parts_x))


def dot(a, b, contract=((1,), (0,)), precision=None):
    return lax.dot_general(a, b, (contract, ((), ())), precision=precision, preferred_element_type=F32)


def split(value):
    high = value.astype(BF16)
    return high, (value - high.astype(F32)).astype(BF16)


def iota(shape, dim):
    return lax.broadcasted_iota(jnp.int32, shape, dim)


def kernel(parts, volume, x_hbm, v_hbm, out_hbm, xp, yp, y2, rem, pot, ypack, yrecv, zpack, zrecv, zcorr,
           high, low, acc, place, buf_x, buf_y, buf_z, part, outv,
           load_sem, send_sem, recv_sem, y2_send, y2_recv, oo_send, oo_recv, ar_send, ar_recv, out_sem):
    count, cx, cy, cz = y2.shape
    nx, ny, nz = parts
    sizes = (nx, ny, nz)
    strides = (ny * nz, nz, 1)
    grid_index = lax.axis_index("grid")
    band = lax.axis_index("band")
    pos = (grid_index // (ny * nz), grid_index // nz % ny, grid_index % nz)
    rows = count * cy
    tiles = cy // 8
    per_pack = cz // SLOT

    def loads(o):
        return pltpu.make_async_copy(
            x_hbm.at[0, o], xp.at[o, REACH:REACH + cx, LEAD:LEAD + cy], load_sem.at[o])

    pot_load = pltpu.make_async_copy(v_hbm.at[0], pot, load_sem.at[count])
    pot_load.start()

    @pl.loop(0, count)
    def _(o):
        loads(o).start()

    barrier = pltpu.get_barrier_semaphore()

    def line_peer(dim, k):
        return grid_index + (lax.rem(pos[dim] + k, sizes[dim]) - pos[dim]) * strides[dim]

    for dim in range(3):
        for k in range(1, sizes[dim]):
            pl.semaphore_signal(barrier, inc=1, device_id={"grid": line_peer(dim, k)}, device_id_type=MESH)
    pl.semaphore_signal(barrier, inc=1, device_id={"band": 1 - band}, device_id_type=MESH)
    pl.semaphore_wait(barrier, nx + ny + nz - 2)

    can_send = []
    for dim in range(3):
        can_send += [pos[dim] < sizes[dim] - 1, pos[dim] > 0]
    can_recv = [can_send[1], can_send[0], can_send[3], can_send[2], can_send[5], can_send[4]]

    def face(stage, o, d):
        field = (xp, yp)[stage]
        if d == 0:
            src, dst = field.at[o, cx:cx + REACH, LEAD:LEAD + cy], field.at[o, 0:REACH, LEAD:LEAD + cy]
        elif d == 1:
            src = field.at[o, REACH:2 * REACH, LEAD:LEAD + cy]
            dst = field.at[o, cx + REACH:cx + 2 * REACH, LEAD:LEAD + cy]
        elif d < 4:
            src, dst = ypack.at[stage, o, d - 2], yrecv.at[stage, o, d - 2]
        else:
            src, dst = zpack.at[stage, o], zrecv.at[stage, o, d - 4]
        step = strides[d // 2] * (1 - 2 * (d % 2))
        return pltpu.make_async_remote_copy(
            src_ref=src, dst_ref=dst, send_sem=send_sem.at[stage, o, d], recv_sem=recv_sem.at[stage, o, d],
            device_id={"grid": grid_index + step}, device_id_type=MESH)

    for d in range(6):
        @pl.when(jnp.logical_not(can_recv[d]))
        def _(d=d):
            @pl.loop(0, 2 * count)
            def _(i):
                stage, o = i // count, i % count
                if d < 2:
                    start = (0, cx + REACH)[d]
                    for k in range(REACH):
                        zero = jnp.zeros((cy, cz), F32)

                        @pl.when(stage == 0)
                        def _():
                            xp[o, start + k, LEAD:LEAD + cy, :] = zero

                        @pl.when(stage == 1)
                        def _():
                            yp[o, start + k, LEAD:LEAD + cy, :] = zero
                elif d < 4:
                    yrecv[stage, o, d - 2] = jnp.zeros(yrecv.shape[3:], F32)
                else:
                    zrecv[stage, o, d - 4] = jnp.zeros(zrecv.shape[3:], F32)

    def pack_y(stage, field, o):
        for x in range(cx):
            ypack[stage, o, 0, REACH * x:REACH * (x + 1), :] = field[o, REACH + x, LEAD + cy - REACH:LEAD + cy, :]
            ypack[stage, o, 1, REACH * x:REACH * (x + 1), :] = field[o, REACH + x, LEAD:LEAD + REACH, :]

    def unpack_y(stage, field, o):
        for x in range(cx):
            field[o, REACH + x, LEAD - REACH:LEAD, :] = yrecv[stage, o, 0, REACH * x:REACH * (x + 1), :]
            field[o, REACH + x, LEAD + cy:LEAD + cy + REACH, :] = yrecv[stage, o, 1, REACH * x:REACH * (x + 1), :]

    lane = iota((8, cz), 1)
    lane_slot = lane // SLOT

    def pack_z_tile(stage, o, x0, y0, values):
        group, slot = x0 // per_pack, x0 % per_pack
        packed = zpack[stage, o, group, pl.ds(y0, 8), :]
        for u, value in enumerate(values):
            turned = pltpu.roll(value, (slot + u) * SLOT + REACH, 1)
            packed = jnp.where(lane_slot == slot + u, turned, packed)
        zpack[stage, o, group, pl.ds(y0, 8), :] = packed

    def correct_z(stage, o):
        own = zpack[stage, o]
        lanes = iota(own.shape, 2) % SLOT
        from_left = jnp.where(lanes < REACH, zrecv[stage, o, 0] - own, 0.0).reshape(-1, cz)
        right = (lanes >= REACH) & (lanes < 2 * REACH)
        from_right = jnp.where(right, zrecv[stage, o, 1] - own, 0.0).reshape(-1, cz)
        low_side, high_side = 0.0, 0.0
        for r in range(1, REACH + 1):
            low_side = low_side + TAPS[r] * pltpu.roll(from_left, r, 1)
            high_side = high_side + TAPS[r] * pltpu.roll(from_right, cz - r, 1)
        low_side, high_side = low_side.reshape(own.shape), high_side.reshape(own.shape)
        zcorr[...] = jnp.where(lanes < REACH, high_side, jnp.where(right, low_side, 0.0))

    edge = (lane < REACH) | (lane >= cz - REACH)

    def stencil_tile(field, o, x0, t):
        y0 = 8 * t
        window = [field[o, x0 + i, LEAD + y0:LEAD + y0 + 8, :] for i in range(UNROLL + 2 * REACH)]
        results = []
        group, slot = x0 // per_pack, x0 % per_pack
        corr = zcorr[group, y0:y0 + 8, :]
        for u in range(UNROLL):
            center = window[u + REACH]
            total = pot[x0 + u, y0:y0 + 8, :] * center
            for r in range(1, REACH + 1):
                pair = window[u + REACH + r] + window[u + REACH - r]
                up = field[o, x0 + u + REACH, LEAD + y0 + r:LEAD + y0 + r + 8, :]
                down = field[o, x0 + u + REACH, LEAD + y0 - r:LEAD + y0 - r + 8, :]
                turned = pltpu.roll(center, r, 1) + pltpu.roll(center, cz - r, 1)
                total = total + TAPS[r] * ((pair + turned) + (up + down))
            fix = pltpu.roll(corr, cz - (slot + u) * SLOT - REACH, 1)
            results.append(total + jnp.where(edge, fix, 0.0))
        return results

    def start_faces(stage, o):
        for d in range(6):
            @pl.when(can_send[d])
            def _(d=d):
                face(stage, o, d).start()

    def wait_faces(stage, o):
        for d in range(6):
            @pl.when(can_recv[d])
            def _(d=d):
                face(stage, o, d).wait_recv()

    @pl.loop(0, count)
    def _(o):
        loads(o).wait()
        pack_y(0, xp, o)

        @pl.loop(0, cx // UNROLL)
        def _(g):
            x0 = g * UNROLL
            for t in range(tiles):
                pack_z_tile(0, o, x0, 8 * t,
                            [xp[o, x0 + u + REACH, LEAD + 8 * t:LEAD + 8 * t + 8, :] for u in range(UNROLL)])

        start_faces(0, o)

    pot_load.wait()

    @pl.loop(0, cx)
    def _(x):
        pot[x] = (pot[x] + DIAGONAL) * (1.0 / HALF_WIDTH)

    @pl.loop(0, count)
    def _(o):
        wait_faces(0, o)
        unpack_y(0, xp, o)
        correct_z(0, o)

        @pl.loop(0, cx // UNROLL)
        def _(g):
            x0 = g * UNROLL
            for t in range(tiles):
                values = stencil_tile(xp, o, x0, t)
                for u in range(UNROLL):
                    yp[o, x0 + u + REACH, LEAD + 8 * t:LEAD + 8 * t + 8, :] = values[u]
                pack_z_tile(1, o, x0, 8 * t, values)

        pack_y(1, yp, o)
        start_faces(1, o)

    def hand_over(o):
        return pltpu.make_async_remote_copy(
            src_ref=y2.at[o], dst_ref=rem.at[o], send_sem=y2_send.at[o], recv_sem=y2_recv.at[o],
            device_id={"band": 1 - band}, device_id_type=MESH)

    @pl.loop(0, count)
    def _(o):
        wait_faces(1, o)
        unpack_y(1, yp, o)
        correct_z(1, o)

        @pl.loop(0, cx // UNROLL)
        def _(g):
            x0 = g * UNROLL
            for t in range(tiles):
                values = stencil_tile(yp, o, x0, t)
                for u in range(UNROLL):
                    start = xp[o, x0 + u + REACH, LEAD + 8 * t:LEAD + 8 * t + 8, :]
                    y2[o, x0 + u, 8 * t:8 * t + 8, :] = (values[u] + values[u]) - start

        hand_over(o).start()

    def wide(ref, x0):
        return jnp.concatenate([ref[:, x0 + u].reshape(rows, cz) for u in range(UNROLL)], axis=1)

    def split_block(which, field, x0):
        for u in range(UNROLL):
            high[which, :, x0 + u], low[which, :, x0 + u] = split(field[:, x0 + u])

    def gram(which):
        acc[...] = jnp.zeros_like(acc)

        @pl.loop(0, cx // UNROLL)
        def _(g):
            x0 = g * UNROLL
            split_block(which, (y2, rem)[which], x0)
            left_high, left_low = wide(high.at[0], x0), wide(low.at[0], x0)
            right_high, right_low = wide(high.at[which], x0), wide(low.at[which], x0)
            inner = ((1,), (1,))
            acc[...] += (dot(left_high, right_high, inner) + dot(left_high, right_low, inner)
                         + dot(left_low, right_high, inner))

    same_y = (iota((rows, rows), 0) % cy) == (iota((rows, rows), 1) % cy)

    def row_pick(which):
        own = jnp.where(which == 0, band, 1 - band) * count
        return (iota((2 * count, rows), 0) == iota((2 * count, rows), 1) // cy + own).astype(F32)

    def column_pick(which):
        own = jnp.where(which == 0, band, 1 - band) * count
        return (iota((rows, cz), 1) == iota((rows, cz), 0) // cy + own).astype(F32)

    gram(0)
    masked = jnp.where(same_y, acc[...], 0.0)
    place[0] = dot(dot(row_pick(0), masked, precision=HIGHEST), column_pick(0), precision=HIGHEST)
    oo_copy = pltpu.make_async_remote_copy(
        src_ref=place.at[0], dst_ref=place.at[1], send_sem=oo_send, recv_sem=oo_recv,
        device_id={"band": 1 - band}, device_id_type=MESH)
    oo_copy.start()

    @pl.loop(0, count)
    def _(o):
        hand_over(o).wait_recv()

    gram(1)
    masked = jnp.where(same_y, acc[...], 0.0)
    cross = dot(dot(row_pick(0), masked, precision=HIGHEST), column_pick(1), precision=HIGHEST)
    flipped = dot(dot(row_pick(1), masked, ((1,), (1,)), HIGHEST), column_pick(0), precision=HIGHEST)
    oo_copy.wait_recv()
    total = place[0] + place[1] + cross + flipped

    buffers = (buf_x, buf_y, buf_z)

    def reduce_copy(dim, k):
        return pltpu.make_async_remote_copy(
            src_ref=part.at[dim], dst_ref=buffers[dim].at[pos[dim]],
            send_sem=ar_send.at[dim, k], recv_sem=ar_recv.at[dim, k],
            device_id={"grid": line_peer(dim, k)}, device_id_type=MESH)

    for dim in (2, 1, 0):
        part[dim] = total
        buffers[dim][pos[dim]] = total
        for k in range(1, sizes[dim]):
            reduce_copy(dim, k).start()
        for k in range(1, sizes[dim]):
            reduce_copy(dim, k).wait_recv()
        total = buffers[dim][0]
        for k in range(1, sizes[dim]):
            total = total + buffers[dim][k]

    orbs = 2 * count
    row_id, lane_id = iota((orbs, cz), 0), iota((orbs, cz), 1)
    work = jnp.where(lane_id < orbs, total * (1.0 / volume), (lane_id == row_id + orbs).astype(F32))
    for k in range(orbs):
        scale = 1.0 / jnp.sqrt(work[k:k + 1, k:k + 1])
        pivot = work[k:k + 1, :] * scale
        column = jnp.where(row_id > k, work[:, k:k + 1] * scale, 0.0)
        work = jnp.where(row_id == k, pivot, work - column * pivot)

    def spread(which):
        own = jnp.where(which == 0, band, 1 - band) * count
        rows_pick = (iota((rows, orbs), 1) == iota((rows, orbs), 0) // cy + band * count).astype(F32)
        lanes_pick = (iota((cz, rows), 0) == iota((cz, rows), 1) // cy + own + orbs).astype(F32)
        full = dot(dot(rows_pick, work, precision=HIGHEST), lanes_pick, precision=HIGHEST)
        return split(jnp.where(same_y, full, 0.0))

    own_high, own_low = spread(0)
    far_high, far_low = spread(1)

    def store(x0):
        return pltpu.make_async_copy(
            outv.at[:, pl.ds(x0, UNROLL)], out_hbm.at[0, :, pl.ds(x0, UNROLL)], out_sem.at[x0 // UNROLL])

    @pl.loop(0, cx // UNROLL)
    def _(g):
        x0 = g * UNROLL
        a_high, a_low = wide(high.at[0], x0), wide(low.at[0], x0)
        b_high, b_low = wide(high.at[1], x0), wide(low.at[1], x0)
        result = (dot(own_high, a_high) + dot(own_high, a_low) + dot(own_low, a_high)
                  + dot(far_high, b_high) + dot(far_high, b_low) + dot(far_low, b_high))
        for u in range(UNROLL):
            outv[:, x0 + u] = result[:, u * cz:(u + 1) * cz].reshape(count, cy, cz)
        store(x0).start()

    @pl.loop(0, cx // UNROLL)
    def _(g):
        store(g * UNROLL).wait()

    @pl.loop(0, count)
    def _(o):
        for stage in range(2):
            for d in range(6):
                @pl.when(can_send[d])
                def _(stage=stage, d=d):
                    face(stage, o, d).wait_send()
        hand_over(o).wait_send()

    oo_copy.wait_send()
    for dim in range(3):
        for k in range(1, sizes[dim]):
            reduce_copy(dim, k).wait_send()


def on_device(orbitals, potential):
    _, count, cx, cy, cz = orbitals.shape
    devices_grid = lax.axis_size("grid")
    parts = layout(devices_grid)
    volume = cx * cy * cz * devices_grid
    rows, orbs = count * cy, 2 * count
    groups = cx * SLOT // cz
    padded = (count, cx + 2 * REACH, cy + 2 * LEAD, cz)
    block = (count, cx, cy, cz)
    dma = pltpu.SemaphoreType.DMA
    most = max(parts)
    any_spec = pl.BlockSpec(memory_space=pl.ANY)
    return pl.pallas_call(
        functools.partial(kernel, parts, volume),
        out_shape=jax.ShapeDtypeStruct(orbitals.shape, F32),
        in_specs=[any_spec, any_spec],
        out_specs=any_spec,
        scratch_shapes=[
            pltpu.VMEM(padded, F32), pltpu.VMEM(padded, F32),
            pltpu.VMEM(block, F32), pltpu.VMEM(block, F32), pltpu.VMEM((cx, cy, cz), F32),
            pltpu.VMEM((2, count, 2, REACH * cx, cz), F32), pltpu.VMEM((2, count, 2, REACH * cx, cz), F32),
            pltpu.VMEM((2, count, groups, cy, cz), F32), pltpu.VMEM((2, count, 2, groups, cy, cz), F32),
            pltpu.VMEM((groups, cy, cz), F32),
            pltpu.VMEM((2,) + block, BF16), pltpu.VMEM((2,) + block, BF16),
            pltpu.VMEM((rows, rows), F32), pltpu.VMEM((2, orbs, cz), F32),
            pltpu.VMEM((parts[0], orbs, cz), F32), pltpu.VMEM((parts[1], orbs, cz), F32),
            pltpu.VMEM((parts[2], orbs, cz), F32), pltpu.VMEM((3, orbs, cz), F32),
            pltpu.VMEM(block, F32),
            dma((count + 1,)), dma((2, count, 6)), dma((2, count, 6)), dma((count,)), dma((count,)),
            dma, dma, dma((3, most)), dma((3, most)), dma((cx // UNROLL,)),
        ],
        compiler_params=pltpu.CompilerParams(
            collective_id=0, has_side_effects=True, vmem_limit_bytes=60 * 1024 * 1024),
    )(orbitals, potential)


def solution(mesh):
    in_specs = (P("grid", "band", None, None, None), P("grid", None, None, None))
    out_specs = P("grid", "band", None, None, None)
    return jax.shard_map(
        on_device, mesh=mesh, in_specs=in_specs, out_specs=out_specs, check_vma=False
    )
```

time: 986 us -> 77.5 us (0.08); the launches traced: 976 us -> 77.4 us
  local copies, waits for them, and re-layouts: 699 us -> 4.64 us
  other arithmetic: 130 us -> 0 us
  Pallas kernels: 0 us -> 72.8 us
  blocking collectives: 42.7 us -> 0 us
  starting transfers between devices: 38.6 us -> 0 us
  matrix products: 25.8 us -> 0 us
  waiting for transfers between devices: 24.7 us -> 0 us
  between operations: 14.2 us -> 0.01 us
    dynamic_update_slice x12 -> x0, local copies, waits for them, and re-layouts: 526 us -> none  [the longest x6 398 us: apply_hamil(): padded = lax.dynamic_update_slice(padded, upper_face, upper_start)]
    reshape x16 -> x0, local copies, waits for them, and re-layouts: 80.8 us -> none  [the longest x8 65.9 us: neighbour(): return jnp.where(keep_it, moved, 0.0).reshape(face_block.shape)]
    pallas_call x0 -> x1, Pallas kernels: none -> 72.8 us  [on_device(): pl.pallas_call(functools.partial(kernel, parts, volume), out_shape=jax.Sh...]
    sub x1 -> x0, other arithmetic: 62.5 us -> none  [chebyshev(): 2.0 * (apply_hamil(first_term, local_potential) - CENTER * first_term)]
    div x3 -> x0, other arithmetic: 61.8 us -> none  [the longest x1 61.8 us: chebyshev(): (apply_hamil(start_block, local_potential) - CENTER * start_block) / HALF...]
    slice x10 -> x0, local copies, waits for them, and re-layouts: 53 us -> none  [the longest x8 36 us: apply_hamil(): lax.slice_in_dim(values_in, 0, reach_max, axis=dim_index)]
    psum x1 -> x0, blocking collectives: 42.7 us -> none  [on_device(): gram = lax.psum(partial_value, 'grid')]
    ppermute x12 -> x0, starting transfers between devices: 38.6 us -> none  [shifted(): lax.ppermute(value, axis, [(source, source + steps) for source in range(l...]
  transfers between devices with their start and end apart: 13 -> 0, of which waited for: 1 -> 0; matrix products, arithmetic and copies ran while one was open for 24% -> 0% of each run, Pallas kernels for 0% -> 0%
where the time goes in v1:
time: 77.5 us; the launch traced here: 77.4 us
  Pallas kernels  72.8 us (94%)
  local copies, waits for them, and re-layouts  4.64 us (6%)
    pallas_call x1, Pallas kernels, on_device(): pl.pallas_call(functools.partial(kernel, parts, volume), out_shape=jax.Sh...  72.8 us
    unnamed x1, local copies, waits for them, and re-layouts  4.64 us

profile of v1, /device:TPU:0, one launch (start us, length us, event | category | flops | bytes accessed | tf_op | source)
XLA Modules:
  0.0 77.4 jit_solution(18350055085183503350)
XLA Ops:
  0.0 72.8 %shard_map.28 = f32[1,8,32,32,128]{4,3,2,1,0:T(8,128)} custom-call(f32[1,8,32,32,128]{4,3,2,1,0:T(8,128)} %x_hbm.1, f32[1,32,32,128]{3,2,1,0:T(8,128)} %v_hbm.1), custom_call_target="tpu_custom_call" | custom-call | tf_op jit(solution)/shard_map/pallas_call | solution.py:382
  72.8 4.6 %copy.4 = f32[1,8,32,32,128]{4,3,2,1,0:T(8,128)} copy(f32[1,8,32,32,128]{4,3,2,1,0:T(8,128)} %shard_map.28) | data formatting | bytes 8388608

commit v2 on v1

--- a/solution.py
+++ b/solution.py
@@ -40,11 +40,12 @@
 
 
 def kernel(parts, volume, x_hbm, v_hbm, out_hbm, xp, yp, y2, rem, pot, ypack, yrecv, zpack, zrecv, zcorr,
-           high, low, acc, place, buf_x, buf_y, buf_z, part, outv,
+           high, low, acc, place, sums, outv,
            load_sem, send_sem, recv_sem, y2_send, y2_recv, oo_send, oo_recv, ar_send, ar_recv, out_sem):
     count, cx, cy, cz = y2.shape
     nx, ny, nz = parts
     sizes = (nx, ny, nz)
+    devices_grid = nx * ny * nz
     strides = (ny * nz, nz, 1)
     grid_index = lax.axis_index("grid")
     band = lax.axis_index("band")
@@ -66,14 +67,15 @@
 
     barrier = pltpu.get_barrier_semaphore()
 
-    def line_peer(dim, k):
-        return grid_index + (lax.rem(pos[dim] + k, sizes[dim]) - pos[dim]) * strides[dim]
-
-    for dim in range(3):
-        for k in range(1, sizes[dim]):
-            pl.semaphore_signal(barrier, inc=1, device_id={"grid": line_peer(dim, k)}, device_id_type=MESH)
+    def grid_peer(k):
+        return lax.rem(grid_index + k, devices_grid)
+
+    @pl.loop(1, devices_grid)
+    def _(k):
+        pl.semaphore_signal(barrier, inc=1, device_id={"grid": grid_peer(k)}, device_id_type=MESH)
+
     pl.semaphore_signal(barrier, inc=1, device_id={"band": 1 - band}, device_id_type=MESH)
-    pl.semaphore_wait(barrier, nx + ny + nz - 2)
+    pl.semaphore_wait(barrier, devices_grid)
 
     can_send = []
     for dim in range(3):
@@ -295,24 +297,25 @@
     oo_copy.wait_recv()
     total = place[0] + place[1] + cross + flipped
 
-    buffers = (buf_x, buf_y, buf_z)
-
-    def reduce_copy(dim, k):
+    sums[grid_index] = total
+
+    def reduce_copy(k):
         return pltpu.make_async_remote_copy(
-            src_ref=part.at[dim], dst_ref=buffers[dim].at[pos[dim]],
-            send_sem=ar_send.at[dim, k], recv_sem=ar_recv.at[dim, k],
-            device_id={"grid": line_peer(dim, k)}, device_id_type=MESH)
-
-    for dim in (2, 1, 0):
-        part[dim] = total
-        buffers[dim][pos[dim]] = total
-        for k in range(1, sizes[dim]):
-            reduce_copy(dim, k).start()
-        for k in range(1, sizes[dim]):
-            reduce_copy(dim, k).wait_recv()
-        total = buffers[dim][0]
-        for k in range(1, sizes[dim]):
-            total = total + buffers[dim][k]
+            src_ref=sums.at[grid_index], dst_ref=sums.at[grid_index],
+            send_sem=ar_send.at[k], recv_sem=ar_recv.at[k],
+            device_id={"grid": grid_peer(k)}, device_id_type=MESH)
+
+    @pl.loop(1, devices_grid)
+    def _(k):
+        reduce_copy(k).start()
+
+    @pl.loop(1, devices_grid)
+    def _(k):
+        reduce_copy(k).wait_recv()
+
+    total = sums[0]
+    for k in range(1, devices_grid):
+        total = total + sums[k]
 
     orbs = 2 * count
     row_id, lane_id = iota((orbs, cz), 0), iota((orbs, cz), 1)
@@ -362,9 +365,10 @@
         hand_over(o).wait_send()
 
     oo_copy.wait_send()
-    for dim in range(3):
-        for k in range(1, sizes[dim]):
-            reduce_copy(dim, k).wait_send()
+
+    @pl.loop(1, devices_grid)
+    def _(k):
+        reduce_copy(k).wait_send()
 
 
 def on_device(orbitals, potential):
@@ -377,7 +381,6 @@
     padded = (count, cx + 2 * REACH, cy + 2 * LEAD, cz)
     block = (count, cx, cy, cz)
     dma = pltpu.SemaphoreType.DMA
-    most = max(parts)
     any_spec = pl.BlockSpec(memory_space=pl.ANY)
     return pl.pallas_call(
         functools.partial(kernel, parts, volume),
@@ -392,11 +395,10 @@
             pltpu.VMEM((groups, cy, cz), F32),
             pltpu.VMEM((2,) + block, BF16), pltpu.VMEM((2,) + block, BF16),
             pltpu.VMEM((rows, rows), F32), pltpu.VMEM((2, orbs, cz), F32),
-            pltpu.VMEM((parts[0], orbs, cz), F32), pltpu.VMEM((parts[1], orbs, cz), F32),
-            pltpu.VMEM((parts[2], orbs, cz), F32), pltpu.VMEM((3, orbs, cz), F32),
+            pltpu.VMEM((devices_grid, orbs, cz), F32),
             pltpu.VMEM(block, F32),
             dma((count + 1,)), dma((2, count, 6)), dma((2, count, 6)), dma((count,)), dma((count,)),
-            dma, dma, dma((3, most)), dma((3, most)), dma((cx // UNROLL,)),
+            dma, dma, dma((devices_grid,)), dma((devices_grid,)), dma((cx // UNROLL,)),
         ],
         compiler_params=pltpu.CompilerParams(
             collective_id=0, has_side_effects=True, vmem_limit_bytes=60 * 1024 * 1024),

time: 77.5 us -> 73.9 us (0.954)
  Pallas kernels: 72.8 us -> 69.1 us
    pallas_call x1, Pallas kernels: 72.8 us -> 69.1 us  [on_device(): pl.pallas_call(functools.partial(kernel, parts, volume), out_shape=jax.Sh...]
where the time goes in v2:
time: 73.9 us; the launch traced here: 73.7 us
  Pallas kernels  69.1 us (94%)
  local copies, waits for them, and re-layouts  4.64 us (6%)
    pallas_call x1, Pallas kernels, on_device(): pl.pallas_call(functools.partial(kernel, parts, volume), out_shape=jax.Sh...  69.1 us
    unnamed x1, local copies, waits for them, and re-layouts  4.64 us

profile of v2, /device:TPU:0, one launch (start us, length us, event | category | flops | bytes accessed | tf_op | source)
XLA Modules:
  0.0 73.7 jit_solution(16184038444953348802)
XLA Ops:
  0.0 69.1 %shard_map.28 = f32[1,8,32,32,128]{4,3,2,1,0:T(8,128)} custom-call(f32[1,8,32,32,128]{4,3,2,1,0:T(8,128)} %x_hbm.1, f32[1,32,32,128]{3,2,1,0:T(8,128)} %v_hbm.1), custom_call_target="tpu_custom_call" | custom-call | tf_op jit(solution)/shard_map/pallas_call | solution.py:385
  69.1 4.6 %copy.4 = f32[1,8,32,32,128]{4,3,2,1,0:T(8,128)} copy(f32[1,8,32,32,128]{4,3,2,1,0:T(8,128)} %shard_map.28) | data formatting | bytes 8388608

commit v3 on v2

--- a/solution.py
+++ b/solution.py
@@ -40,7 +40,7 @@
 
 
 def kernel(parts, volume, x_hbm, v_hbm, out_hbm, xp, yp, y2, rem, pot, ypack, yrecv, zpack, zrecv, zcorr,
-           high, low, acc, place, sums, outv,
+           high, low, acc, place, sums, band_z, outv,
            load_sem, send_sem, recv_sem, y2_send, y2_recv, oo_send, oo_recv, ar_send, ar_recv, out_sem):
     count, cx, cy, cz = y2.shape
     nx, ny, nz = parts
@@ -157,7 +157,12 @@
 
     edge = (lane < REACH) | (lane >= cz - REACH)
 
-    def stencil_tile(field, o, x0, t):
+    def along_z(field, o, x0):
+        start = field[o, pl.ds(x0 + REACH, UNROLL), LEAD:LEAD + cy, :].reshape(UNROLL * cy, cz)
+        both = dot(jnp.concatenate(split(start), axis=1), band_z[...])
+        return both[:, :cz] + both[:, cz:]
+
+    def stencil_tile(field, o, x0, t, turned):
         y0 = 8 * t
         window = [field[o, x0 + i, LEAD + y0:LEAD + y0 + 8, :] for i in range(UNROLL + 2 * REACH)]
         results = []
@@ -165,19 +170,18 @@
         corr = zcorr[group, y0:y0 + 8, :]
         for u in range(UNROLL):
             center = window[u + REACH]
-            total = pot[x0 + u, y0:y0 + 8, :] * center
+            total = pot[x0 + u, y0:y0 + 8, :] * center + turned[u * cy + y0:u * cy + y0 + 8]
             for r in range(1, REACH + 1):
                 pair = window[u + REACH + r] + window[u + REACH - r]
                 up = field[o, x0 + u + REACH, LEAD + y0 + r:LEAD + y0 + r + 8, :]
                 down = field[o, x0 + u + REACH, LEAD + y0 - r:LEAD + y0 - r + 8, :]
-                turned = pltpu.roll(center, r, 1) + pltpu.roll(center, cz - r, 1)
-                total = total + TAPS[r] * ((pair + turned) + (up + down))
+                total = total + TAPS[r] * (pair + (up + down))
             fix = pltpu.roll(corr, cz - (slot + u) * SLOT - REACH, 1)
             results.append(total + jnp.where(edge, fix, 0.0))
         return results
 
-    def start_faces(stage, o):
-        for d in range(6):
+    def start_faces(stage, o, sides=tuple(range(6))):
+        for d in sides:
             @pl.when(can_send[d])
             def _(d=d):
                 face(stage, o, d).start()
@@ -191,7 +195,9 @@
     @pl.loop(0, count)
     def _(o):
         loads(o).wait()
+        start_faces(0, o, (0, 1))
         pack_y(0, xp, o)
+        start_faces(0, o, (2, 3))
 
         @pl.loop(0, cx // UNROLL)
         def _(g):
@@ -200,8 +206,17 @@
                 pack_z_tile(0, o, x0, 8 * t,
                             [xp[o, x0 + u + REACH, LEAD + 8 * t:LEAD + 8 * t + 8, :] for u in range(UNROLL)])
 
-        start_faces(0, o)
-
+        start_faces(0, o, (4, 5))
+
+    apart = jnp.abs(iota((cz, cz), 0) - iota((cz, cz), 1))
+    weights = jnp.zeros((cz, cz), F32)
+    for r in range(1, REACH + 1):
+        weights = jnp.where((apart == r) | (apart == cz - r), TAPS[r], weights)
+    weights_high, weights_low = split(weights)
+    band_z[0:cz, 0:cz] = weights_high
+    band_z[0:cz, cz:2 * cz] = weights_low
+    band_z[cz:2 * cz, 0:cz] = weights_high
+    band_z[cz:2 * cz, cz:2 * cz] = jnp.zeros((cz, cz), BF16)
     pot_load.wait()
 
     @pl.loop(0, cx)
@@ -217,14 +232,16 @@
         @pl.loop(0, cx // UNROLL)
         def _(g):
             x0 = g * UNROLL
+            turned = along_z(xp, o, x0)
             for t in range(tiles):
-                values = stencil_tile(xp, o, x0, t)
+                values = stencil_tile(xp, o, x0, t, turned)
                 for u in range(UNROLL):
                     yp[o, x0 + u + REACH, LEAD + 8 * t:LEAD + 8 * t + 8, :] = values[u]
                 pack_z_tile(1, o, x0, 8 * t, values)
 
+        start_faces(1, o, (0, 1, 4, 5))
         pack_y(1, yp, o)
-        start_faces(1, o)
+        start_faces(1, o, (2, 3))
 
     def hand_over(o):
         return pltpu.make_async_remote_copy(
@@ -240,8 +257,9 @@
         @pl.loop(0, cx // UNROLL)
         def _(g):
             x0 = g * UNROLL
+            turned = along_z(yp, o, x0)
             for t in range(tiles):
-                values = stencil_tile(yp, o, x0, t)
+                values = stencil_tile(yp, o, x0, t, turned)
                 for u in range(UNROLL):
                     start = xp[o, x0 + u + REACH, LEAD + 8 * t:LEAD + 8 * t + 8, :]
                     y2[o, x0 + u, 8 * t:8 * t + 8, :] = (values[u] + values[u]) - start
@@ -265,8 +283,8 @@
             left_high, left_low = wide(high.at[0], x0), wide(low.at[0], x0)
             right_high, right_low = wide(high.at[which], x0), wide(low.at[which], x0)
             inner = ((1,), (1,))
-            acc[...] += (dot(left_high, right_high, inner) + dot(left_high, right_low, inner)
-                         + dot(left_low, right_high, inner))
+            acc[...] += dot(jnp.concatenate([left_high, left_high, left_low], axis=1),
+                            jnp.concatenate([right_high, right_low, right_high], axis=1), inner)
 
     same_y = (iota((rows, rows), 0) % cy) == (iota((rows, rows), 1) % cy)
 
@@ -395,7 +413,7 @@
             pltpu.VMEM((groups, cy, cz), F32),
             pltpu.VMEM((2,) + block, BF16), pltpu.VMEM((2,) + block, BF16),
             pltpu.VMEM((rows, rows), F32), pltpu.VMEM((2, orbs, cz), F32),
-            pltpu.VMEM((devices_grid, orbs, cz), F32),
+            pltpu.VMEM((devices_grid, orbs, cz), F32), pltpu.VMEM((2 * cz, 2 * cz), BF16),
             pltpu.VMEM(block, F32),
             dma((count + 1,)), dma((2, count, 6)), dma((2, count, 6)), dma((count,)), dma((count,)),
             dma, dma, dma((devices_grid,)), dma((devices_grid,)), dma((cx // UNROLL,)),

time: 73.9 us -> 72.8 us (0.985)
  Pallas kernels: 69.1 us -> 68 us
    pallas_call x1, Pallas kernels: 69.1 us -> 68 us  [on_device(): pl.pallas_call(functools.partial(kernel, parts, volume), out_shape=jax.Sh...]
where the time goes in v3:
time: 72.8 us; the launch traced here: 72.7 us
  Pallas kernels  68 us (93%)
  local copies, waits for them, and re-layouts  4.64 us (6%)
    pallas_call x1, Pallas kernels, on_device(): pl.pallas_call(functools.partial(kernel, parts, volume), out_shape=jax.Sh...  68 us
    unnamed x1, local copies, waits for them, and re-layouts  4.64 us

profile of v3, /device:TPU:0, one launch (start us, length us, event | category | flops | bytes accessed | tf_op | source)
XLA Modules:
  0.0 72.7 jit_solution(14592415972541275473)
XLA Ops:
  0.0 68.0 %shard_map.28 = f32[1,8,32,32,128]{4,3,2,1,0:T(8,128)} custom-call(f32[1,8,32,32,128]{4,3,2,1,0:T(8,128)} %x_hbm.1, f32[1,32,32,128]{3,2,1,0:T(8,128)} %v_hbm.1), custom_call_target="tpu_custom_call" | custom-call | tf_op jit(solution)/shard_map/pallas_call | solution.py:403
  68.0 4.6 %copy.4 = f32[1,8,32,32,128]{4,3,2,1,0:T(8,128)} copy(f32[1,8,32,32,128]{4,3,2,1,0:T(8,128)} %shard_map.28) | data formatting | bytes 8388608
